TPU v7x, 128 devices: a whole 4x4x4 slice. The times are simulated.
128 devices in a mesh: row: 8 (over z, core), col: 16 (over x, y).
Axes of the slice: x: 4, y: 4, z: 4, core: 2. Of those that a mesh axis runs over, the one named last changes fastest.
Arguments:
- nodes: bfloat16 [65536, 512], P(('row', 'col')), may hold values from -6 to 6
- cotangent: bfloat16 [65536, 512], P(('row', 'col')), may hold values from -6 to 6
- edge_source: int32 [262144], P(('row', 'col')), may hold values from 0 to 639
- edge_target: int32 [262144], P(('row', 'col')), may hold values from 0 to 511
- halo_lists: int32 [128, 4, 32], P(('row', 'col')), may hold values from 0 to 511
- pool_owner: int32 [65536], P(('row', 'col')), may hold values from 0 to 127, as said below
- pool_table: int32 [128, 1024], P(('row', 'col')), may hold values from -1 to 127, as said below
- source_weight: bfloat16 [512, 512], replicated, may hold values from -0.25 to 0.25
- target_weight: bfloat16 [512, 512], replicated, may hold values from -0.25 to 0.25
- edge_weight: bfloat16 [512, 512], replicated, may hold values from -0.25 to 0.25
- inner_weight: bfloat16 [1024, 512], replicated, may hold values from -0.1875 to 0.1875
- outer_weight: bfloat16 [512, 512], replicated, may hold values from -0.25 to 0.25
- coarse_weight: bfloat16 [512, 512], replicated, may hold values from -0.5 to 0.5
Outputs:
- updated: bfloat16 [65536, 512], P(('row', 'col'))
- node_gradient: float32 [65536, 512], P(('row', 'col'))
- source_gradient: float32 [512, 512], replicated
- target_gradient: float32 [512, 512], replicated
- edge_gradient: float32 [512, 512], replicated
- inner_gradient: float32 [1024, 512], replicated
- outer_gradient: float32 [512, 512], replicated
- coarse_gradient: float32 [512, 512], replicated
Inputs may be any that keep to these rules, and one draw needn't show every extreme that they name: `edge_source`: rows below 512 are the partition's own nodes; row 512 + k * 32 + j is row j of halo block k. `pool_owner`: at most 8 nodes of one partition name the same owner; one owner is named by exactly 8 nodes of every partition. `pool_table`: entry [o, q * 8 + k] is the coarse row of owner o for the node of rank k among the nodes of partition q that name o, and -1 where q names o fewer than k + 1 times.
All inputs are finite; a program needn't handle non-finite values.
Results may differ from a plain program's by a relative error of at most 0.014.
Values may be sent and summed in bfloat16 or wider, within the bound.
No kernel may reach another device: no remote copies, remote signals or barrier semaphores. Data moves between devices by JAX's collectives and lax.ppermute only.
A program may use at most 128 MiB of HBM per device.

v0:
```python
import math
import jax
import jax.numpy as jnp
from jax import lax
from jax.sharding import PartitionSpec as P


def passed_along(value, axis, steps):
    count = lax.axis_size(axis)
    initial, last = (max(0, -steps), min(count, count - steps))
    return lax.ppermute(value, axis, [(source, source + steps) for source in range(initial, last)])


def product(first, second):
    return jnp.dot(first, second, preferred_element_type=jnp.float32)


def left_product(first, second):
    return lax.dot_general(
        first, second, (((0,), (0,)), ((), ())), preferred_element_type=jnp.float32
    )


def right_product(first, second):
    return lax.dot_general(
        first, second, (((1,), (1,)), ((), ())), preferred_element_type=jnp.float32
    )


def silu_slope(value):
    sigma = jax.nn.sigmoid(value)
    return sigma * (1.0 + value * (1.0 - sigma))


def trade_halo(blocks, flip):
    moved = []
    for number, offset in enumerate((1, -1)):
        moved.append(passed_along(blocks[number], "row", offset * flip))
    for number, offset in enumerate((1, -1)):
        moved.append(passed_along(blocks[2 + number], "col", offset * flip))
    return moved


def trade_slots(buffer):
    return lax.all_to_all(buffer, ("row", "col"), split_axis=0, concat_axis=0, tiled=True)


def toward_owners(values, slot, devices, capacity, trader):
    width = values.shape[1]
    outgoing = jnp.zeros((devices * capacity, width), values.dtype).at[slot].set(values)
    arrived = trader(outgoing.reshape(devices, capacity, width))
    return arrived.reshape(devices * capacity, width)


def toward_sources(coarse_values, table, slot, devices, capacity, trader):
    width = coarse_values.shape[1]
    picked = jnp.take(coarse_values, jnp.maximum(table, 0), axis=0)
    picked = jnp.where((table >= 0)[:, None], picked, jnp.zeros_like(picked))
    returned = trader(picked.reshape(devices, capacity, width)).reshape(devices * capacity, width)
    return jnp.take(returned, slot, axis=0)


def local(
    nodes,
    cotangent,
    edge_source,
    edge_target,
    halo_lists,
    pool_owner,
    pool_table,
    source_weight,
    target_weight,
    edge_weight,
    inner_weight,
    outer_weight,
    coarse_weight,
):
    devices = lax.axis_size("row") * lax.axis_size("col")
    count_rows, width = nodes.shape
    lists = halo_lists[0]
    halo_rows = lists.shape[1]
    table = pool_table[0]
    capacity = table.shape[0] // devices
    coarse_rows = count_rows // 4
    scale = 1.0 / math.sqrt(count_rows * devices)
    received = trade_halo([jnp.take(nodes, lists[number], axis=0) for number in range(4)], 1)
    extended = jnp.concatenate([nodes] + received, axis=0)
    source_side = product(extended, source_weight)
    target_side = product(nodes, target_weight)
    edge_linear = jnp.take(source_side, edge_source, axis=0) + jnp.take(
        target_side, edge_target, axis=0
    )
    edge_hidden = jax.nn.silu(edge_linear).astype(jnp.bfloat16)
    message_linear = product(edge_hidden, edge_weight)
    aggregate = jax.ops.segment_sum(jax.nn.silu(message_linear), edge_target, count_rows).astype(
        jnp.bfloat16
    )
    joined = jnp.concatenate([nodes, aggregate], axis=1)
    node_linear = product(joined, inner_weight)
    node_hidden = jax.nn.silu(node_linear).astype(jnp.bfloat16)
    refined = (nodes.astype(jnp.float32) + product(node_hidden, outer_weight)).astype(jnp.bfloat16)
    owner_hot = (pool_owner[:, None] == jnp.arange(devices, dtype=jnp.int32)[None, :]).astype(
        jnp.bfloat16
    )
    positions = jnp.arange(count_rows, dtype=jnp.int32)
    lower = (positions[:, None] > positions[None, :]).astype(jnp.bfloat16)
    rank = jnp.sum(product(lower, owner_hot) * owner_hot, axis=1).astype(jnp.int32)
    slot = pool_owner * capacity + rank
    member = (jnp.arange(coarse_rows, dtype=jnp.int32)[:, None] == table[None, :]).astype(
        jnp.bfloat16
    )
    count = jnp.maximum(jnp.sum(member, axis=1, dtype=jnp.float32), 1.0)[:, None]
    arrived = toward_owners(refined, slot, devices, capacity, trade_slots)
    coarse = (product(member, arrived) / count).astype(jnp.bfloat16)
    coarse_linear = product(coarse, coarse_weight)
    coarse_update = jax.nn.silu(coarse_linear).astype(jnp.bfloat16)
    parent_rows = toward_sources(coarse_update, table, slot, devices, capacity, trade_slots)
    arrived_grad = toward_owners(cotangent, slot, devices, capacity, trade_slots)
    grad_coarse = (product(member, arrived_grad) * silu_slope(coarse_linear)).astype(jnp.bfloat16)
    coarse_share = (right_product(grad_coarse, coarse_weight) / count).astype(jnp.bfloat16)
    share_rows = toward_sources(coarse_share, table, slot, devices, capacity, trade_slots)
    updated = (refined.astype(jnp.float32) + parent_rows.astype(jnp.float32)).astype(jnp.bfloat16)
    coarse_gradient = left_product(coarse, grad_coarse)
    grad_refined = cotangent.astype(jnp.float32) + share_rows.astype(jnp.float32)
    refined_low = grad_refined.astype(jnp.bfloat16)
    outer_gradient = left_product(node_hidden, refined_low)
    grad_hidden = (right_product(refined_low, outer_weight) * silu_slope(node_linear)).astype(
        jnp.bfloat16
    )
    inner_gradient = left_product(joined, grad_hidden)
    grad_joined = right_product(grad_hidden, inner_weight)
    grad_aggregate = grad_joined[:, width:].astype(jnp.bfloat16)
    grad_message = (
        jnp.take(grad_aggregate, edge_target, axis=0) * silu_slope(message_linear)
    ).astype(jnp.bfloat16)
    edge_gradient = left_product(edge_hidden, grad_message)
    grad_edges = right_product(grad_message, edge_weight) * silu_slope(edge_linear)
    grad_sources = jax.ops.segment_sum(grad_edges, edge_source, extended.shape[0]).astype(
        jnp.bfloat16
    )
    grad_targets = jax.ops.segment_sum(grad_edges, edge_target, count_rows).astype(jnp.bfloat16)
    source_gradient = left_product(extended, grad_sources)
    target_gradient = left_product(nodes, grad_targets)
    (
        source_gradient,
        target_gradient,
        edge_gradient,
        inner_gradient,
        outer_gradient,
        coarse_gradient,
    ) = lax.psum(
        (
            source_gradient,
            target_gradient,
            edge_gradient,
            inner_gradient,
            outer_gradient,
            coarse_gradient,
        ),
        ("row", "col"),
    )
    grad_extended = right_product(grad_sources, source_weight)
    back_blocks = grad_extended[count_rows:].astype(jnp.bfloat16).reshape(4, halo_rows, width)
    returned = trade_halo([back_blocks[number] for number in range(4)], -1)
    node_gradient = (
        grad_refined
        + grad_joined[:, :width]
        + right_product(grad_targets, target_weight)
        + grad_extended[:count_rows]
    )
    node_gradient = node_gradient.at[lists.reshape(-1)].add(
        jnp.concatenate(returned, axis=0).astype(jnp.float32)
    )
    return (
        updated,
        node_gradient,
        source_gradient * scale,
        target_gradient * scale,
        edge_gradient * scale,
        inner_gradient * scale,
        outer_gradient * scale,
        coarse_gradient * scale,
    )


def solution(mesh):
    in_specs = (
        P(("row", "col"), None),
        P(("row", "col"), None),
        P(("row", "col")),
        P(("row", "col")),
        P(("row", "col"), None, None),
        P(("row", "col")),
        P(("row", "col"), None),
        P(),
        P(),
        P(),
        P(),
        P(),
        P(),
    )
    out_specs = (P(("row", "col"), None), P(("row", "col"), None), P(), P(), P(), P(), P(), P())
    return jax.shard_map(local, mesh=mesh, in_specs=in_specs, out_specs=out_specs, check_vma=False)
```

profile of v0, /device:TPU:1, one launch (start us, length us, event | category | flops | bytes accessed | tf_op | source)
XLA Modules:
  0.0 423.6 jit_solution(16720933355326291041)
XLA Ops:
  8.1 1.7 gather_fusion.3
  9.9 4.9 %collective-permute-start = (bf16[32,512]{1,0:T(8,128)(2,1)S(1)}, bf16[32,512]{1,0:T(8,128)(2,1)S(1)}, u32[]{:S(2)}, u32[]{:S(2)}) collective-permute-start(bf16[32,512]{1,0:T(8,128)(2,1)S(1)} %broadcast_select_fusion.4), channel_id=1, source_target_pairs={{0,16},{16,32},{32,48},{48,64},{64,80},{80,96},{96,112},{1,17},{17... | collective-permute-start | bytes 98312 | tf_op jit(solution)/shard_map/ppermute | solution.py:11
  14.8 1.7 gather_fusion.4
  16.7 1.9 collective-permute-start.1
  18.6 1.7 gather_fusion.5
  20.4 3.2 collective-permute-start.2
  23.6 1.7 gather_fusion.6
  25.5 1.3 collective-permute-start.3
  27.5 1.3 compare_and_fusion
  28.8 1.6 fusion.57
  30.4 1.1 fusion.9
  32.1 8.9 %gather_fusion.1 = f32[2048,512]{1,0:T(8,128)} fusion(f32[512,512]{1,0:T(8,128)S(1)} %fusion.57, s32[2048]{0:T(1024)S(1)} %get-tuple-element.46), kind=kCustom, calls=%fused_computation.9 | custom fusion | bytes 8396800 | tf_op jit(solution)/shard_map/jit(_take)/gather | solution.py:90
  41.1 1.5 fusion.56
  42.6 8.9 %gather_fusion = f32[2048,512]{1,0:T(8,128)} fusion(f32[640,512]{1,0:T(8,128)S(1)} %fusion.56, s32[2048]{0:T(1024)S(1)} %get-tuple-element.45), kind=kCustom, calls=%fused_computation.8 | custom fusion | bytes 8396800 | tf_op jit(solution)/shard_map/jit(_take)/gather | solution.py:90
  51.6 4.2 %multiply_convert_fusion.1 = bf16[2048,512]{1,0:T(8,128)(2,1)S(1)} fusion(f32[2048,512]{1,0:T(8,128)} %gather_fusion.1, pred[2048]{0:T(1024)(128)(4,1)} %get-tuple-element.47, f32[2048,512]{1,0:T(8,128)} %gather_fusion, pred[2048]{0:T(1024)(128)(4,1)} %get-tuple-element.48), kind=kLoop, calls=%fused_computation.22 | loop fusion | flops 8388608 | bytes 10489856 | tf_op jit(solution)/shard_map/convert_element_type | solution.py:93
  55.8 1.3 copy-done.5
  57.1 3.3 fusion.58
  60.4 14.6 %scatter_custom_fusion = f32[512,512]{1,0:T(8,128)S(1)} fusion(s32[2048]{0:T(1024)} %param.22, f32[2048,512]{1,0:T(8,128)} %fusion.58, f32[]{:T(128)} %constant.62.clone.1, f32[]{:T(128)} %constant.52.clone.1), kind=kCustom, calls=%fused_computation.19 | custom fusion | flops 5242880 | bytes 5243904 | tf_op jit(solution)/shard_map/scatter-add | solution.py:95
  77.2 3.6 scatter_custom_fusion.1
  80.8 11.6 %all-to-all-start = ((bf16[128,8,512]{2,1,0:T(8,128)(2,1)}), bf16[128,8,512]{2,1,0:T(8,128)(2,1)S(1)}, u32[]{:S(2)}, u32[]{:S(2)}) async-start(bf16[128,8,512]{2,1,0:T(8,128)(2,1)} %bitcast.5), calls=%async_computation | async-start | bytes 2097152 | tf_op jit(solution)/shard_map/all_to_all | solution.py:45
  92.4 4.0 scatter_custom_fusion.2
  96.4 14.7 %all-to-all-done = bf16[128,8,512]{2,1,0:T(8,128)(2,1)S(1)} async-done(((bf16[128,8,512]{2,1,0:T(8,128)(2,1)}), bf16[128,8,512]{2,1,0:T(8,128)(2,1)S(1)}, u32[]{:S(2)}, u32[]{:S(2)}) %all-to-all-start) | async-done | bytes 1048608 | tf_op jit(solution)/shard_map/all_to_all | solution.py:45
  111.2 5.7 %all-to-all-start.2 = ((bf16[128,8,512]{2,1,0:T(8,128)(2,1)}), bf16[128,8,512]{2,1,0:T(8,128)(2,1)}, u32[]{:S(2)}, u32[]{:S(2)}) async-start(bf16[128,8,512]{2,1,0:T(8,128)(2,1)} %bitcast.9), calls=%async_computation.2 | async-start | bytes 2097152 | tf_op jit(solution)/shard_map/all_to_all | solution.py:45
  117.8 1.4 multiply_convert_fusion.3
  119.2 16.3 %all-to-all-done.2 = bf16[128,8,512]{2,1,0:T(8,128)(2,1)} async-done(((bf16[128,8,512]{2,1,0:T(8,128)(2,1)}), bf16[128,8,512]{2,1,0:T(8,128)(2,1)}, u32[]{:S(2)}, u32[]{:S(2)}) %all-to-all-start.2) | async-done | bytes 1048608 | tf_op jit(solution)/shard_map/all_to_all | solution.py:45
  135.5 1.5 fusion.8
  137.7 1.4 fusion.6
  139.1 4.0 gather_fusion.9
  143.1 5.1 %gather_fusion.7 = bf16[1024,512]{1,0:T(8,128)(2,1)} fusion(bf16[128,512]{1,0:T(8,128)(2,1)S(1)} %get-tuple-element.41, s32[1024]{0:T(1024)S(1)} %maximum_clamp_fusion), kind=kCustom, calls=%fused_computation.1.clone | custom fusion | bytes 2101248 | tf_op jit(solution)/shard_map/jit(_take)/gather | solution.py:57
  148.2 2.9 fusion.12
  151.1 4.8 %all-to-all-start.3 = ((bf16[128,8,512]{2,1,0:T(8,128)(2,1)}), bf16[128,8,512]{2,1,0:T(8,128)(2,1)S(1)}, u32[]{:S(2)}, u32[]{:S(2)}) async-start(bf16[128,8,512]{2,1,0:T(8,128)(2,1)} %get-tuple-element.33), calls=%async_computation.3 | async-start | bytes 2097152 | tf_op jit(solution)/shard_map/all_to_all | solution.py:45
  156.0 2.3 fusion.61
  158.3 16.6 %all-to-all-done.3 = bf16[128,8,512]{2,1,0:T(8,128)(2,1)S(1)} async-done(((bf16[128,8,512]{2,1,0:T(8,128)(2,1)}), bf16[128,8,512]{2,1,0:T(8,128)(2,1)S(1)}, u32[]{:S(2)}, u32[]{:S(2)}) %all-to-all-start.3) | async-done | bytes 1048608 | tf_op jit(solution)/shard_map/all_to_all | solution.py:45
  174.9 2.6 gather_fusion.10
  177.5 2.4 fusion.5
  180.7 1.3 copy-done.8
  182.1 9.2 %gather_fusion.2 = bf16[2048,512]{1,0:T(8,128)(2,1)} fusion(bf16[512,512]{1,0:T(8,128)(2,1)S(1)} %slice.97, s32[2048]{0:T(1024)S(1)} %get-tuple-element.46), kind=kCustom, calls=%fused_computation.10 | custom fusion | bytes 4202496 | tf_op jit(solution)/shard_map/jit(_take)/gather | solution.py:134
  191.3 3.8 multiply_convert_fusion
  195.1 1.3 copy-done.10
  197.4 4.3 %multiply_multiply_fusion = f32[2048,512]{1,0:T(8,128)} fusion(bf16[2048,512]{1,0:T(8,128)(2,1)S(1)} %multiply_convert_fusion, bf16[512,512]{1,0:T(8,128)(2,1)S(1)} %copy-done.20, f32[2048,512]{1,0:T(8,128)S(1)} %copy-done.2, pred[2048]{0:T(1024)(128)(4,1)S(1)} %copy-done.31, f32[2048,512]{1,0:T(8,128)S(1)} %copy-done.3, pred[2048]{0:T(1024)(128)(4,1)S(1)} %copy-done.32), kind=kOutput, calls=%fused_computation.17 | convolution fusion | flops 1085276160 | bytes 15208448 | tf_op jit(solution)/shard_map/dot_general | solution.py:25
  201.6 13.6 %scatter_custom_fusion.4 = f32[640,512]{1,0:T(8,128)S(1)} fusion(s32[2048]{0:T(1024)} %param.21, f32[2048,512]{1,0:T(8,128)} %multiply_multiply_fusion, f32[]{:T(128)} %constant.52.clone.1), kind=kCustom, calls=%fused_computation.59 | custom fusion | flops 1048576 | bytes 1311232 | tf_op jit(solution)/shard_map/scatter-add | solution.py:138
  215.2 13.7 %scatter_custom_fusion.3 = f32[512,512]{1,0:T(8,128)S(1)} fusion(s32[2048]{0:T(1024)} %param.22, f32[2048,512]{1,0:T(8,128)} %multiply_multiply_fusion, f32[]{:T(128)} %constant.52.clone.1), kind=kCustom, calls=%fused_computation.73 | custom fusion | flops 1048576 | bytes 1049088 | tf_op jit(solution)/shard_map/scatter-add | solution.py:141
  229.0 4.9 %fusion.60 = f32[512,512]{1,0:T(8,128)} fusion(bf16[2048,512]{1,0:T(8,128)(2,1)} %copy-done.5, bf16[2048,512]{1,0:T(8,128)(2,1)} %copy-done.10), kind=kOutput, calls=%fused_computation.144 | convolution fusion | flops 1073741824 | bytes 5242880 | tf_op jit(solution)/shard_map/dot_general | solution.py:19
  233.9 2.1 fusion.15
  236.0 1.7 fusion.51
  237.6 1.6 fusion.27
  239.2 1.5 convolution_bitcast_fusion
  240.7 4.7 %all-to-all-start.1 = ((bf16[128,8,512]{2,1,0:T(8,128)(2,1)}), bf16[128,8,512]{2,1,0:T(8,128)(2,1)S(1)}, u32[]{:S(2)}, u32[]{:S(2)}) async-start(bf16[128,8,512]{2,1,0:T(8,128)(2,1)} %get-tuple-element.34), calls=%async_computation.1 | async-start | bytes 2097152 | tf_op jit(solution)/shard_map/all_to_all | solution.py:45
  245.5 22.7 %all-to-all-done.1 = bf16[128,8,512]{2,1,0:T(8,128)(2,1)S(1)} async-done(((bf16[128,8,512]{2,1,0:T(8,128)(2,1)}), bf16[128,8,512]{2,1,0:T(8,128)(2,1)S(1)}, u32[]{:S(2)}, u32[]{:S(2)}) %all-to-all-start.1) | async-done | bytes 1048608 | tf_op jit(solution)/shard_map/all_to_all | solution.py:45
  268.2 2.0 gather_fusion.8
  270.3 1.7 fusion.55
  272.0 2.4 collective-permute-start.7
  274.4 1.3 collective-permute-start.6
  275.7 3.1 collective-permute-start.5
  278.8 1.9 collective-permute-start.4
  280.8 1.6 fusion.3
  284.1 1.8 scatter_custom_fusion.5
  285.9 121.3 %all-reduce.3.cloned.1.call-done = (f32[512,512]{1,0:T(8,128)}, f32[512,512]{1,0:T(8,128)}, f32[512,512]{1,0:T(8,128)}, f32[1024,512]{1,0:T(8,128)}, f32[512,512]{1,0:T(8,128)}, /*index=5*/f32[512,512]{1,0:T(8,128)}) async-done(((f32[512,512]{1,0:T(8,128)}, f32[512,512]{1,0:T(8,128)}, f32[512,512]{1,0:T(8,128)}, f32[1024,512]{1,0:T(8,128)}, f32[512,512]{1,0:T(8,128)}, /*index=5*/f32[512,512]{1,0:T(8,128)}), ...) | async-done | bytes 7340048 | tf_op jit(solution)/shard_map/psum | solution.py:151
  407.2 2.4 broadcast_multiply_fusion.5
  409.6 2.4 broadcast_multiply_fusion.4
  412.0 1.1 broadcast_multiply_fusion.3
  413.1 1.5 broadcast_multiply_fusion
  414.6 1.1 broadcast_multiply_fusion.2
  415.7 1.1 broadcast_multiply_fusion.1
  (126 shorter events, 10.1 us)
Async XLA Ops:
  7.2 68.0 %copy-start = (bf16[1024,512]{1,0:T(8,128)(2,1)S(1)}, bf16[1024,512]{1,0:T(8,128)(2,1)}, u32[]{:S(2)}) copy-start(bf16[1024,512]{1,0:T(8,128)(2,1)} %param.29) | copy-start | bytes 3145732
  7.2 24.9 %copy-start.4 = (bf16[512,512]{1,0:T(8,128)(2,1)S(1)}, bf16[512,512]{1,0:T(8,128)(2,1)}, u32[]{:S(2)}) copy-start(bf16[512,512]{1,0:T(8,128)(2,1)} %param.19) | copy-start | bytes 1572868
  7.2 24.3 %copy-start.39 = (s32[512]{0:T(512)S(1)}, s32[512]{0:T(512)}, u32[]{:S(2)}) copy-start(s32[512]{0:T(512)} %param.24) | copy-start | bytes 6148
  9.9 31.1 %collective-permute-start = (bf16[32,512]{1,0:T(8,128)(2,1)S(1)}, bf16[32,512]{1,0:T(8,128)(2,1)S(1)}, u32[]{:S(2)}, u32[]{:S(2)}) collective-permute-start(bf16[32,512]{1,0:T(8,128)(2,1)S(1)} %broadcast_select_fusion.4), channel_id=1, source_target_pairs={{0,16},{16,32},{32,48},{48,64},{64,80},{80,96},{96,112},{1,17},{17... | collective-permute-start | bytes 98312 | tf_op jit(solution)/shard_map/ppermute | solution.py:11
  16.7 24.4 %collective-permute-start.1 = (bf16[32,512]{1,0:T(8,128)(2,1)S(1)}, bf16[32,512]{1,0:T(8,128)(2,1)S(1)}, u32[]{:S(2)}, u32[]{:S(2)}) collective-permute-start(bf16[32,512]{1,0:T(8,128)(2,1)S(1)} %broadcast_select_fusion.3), channel_id=1, source_target_pairs={{16,0},{32,16},{48,32},{64,48},{80,64},{96,80},{112,96},{17,1},{33... | collective-permute-start | bytes 98312 | tf_op jit(solution)/shard_map/ppermute | solution.py:11
  20.4 20.6 %collective-permute-start.2 = (bf16[32,512]{1,0:T(8,128)(2,1)S(1)}, bf16[32,512]{1,0:T(8,128)(2,1)S(1)}, u32[]{:S(2)}, u32[]{:S(2)}) collective-permute-start(bf16[32,512]{1,0:T(8,128)(2,1)S(1)} %broadcast_select_fusion.2), channel_id=1, source_target_pairs={{0,1},{1,2},{2,3},{3,4},{4,5},{5,6},{6,7},{7,8},{8,9},{9,10},{10,1... | collective-permute-start | bytes 98312 | tf_op jit(solution)/shard_map/ppermute | solution.py:11
  25.5 15.6 %collective-permute-start.3 = (bf16[32,512]{1,0:T(8,128)(2,1)S(1)}, bf16[32,512]{1,0:T(8,128)(2,1)S(1)}, u32[]{:S(2)}, u32[]{:S(2)}) collective-permute-start(bf16[32,512]{1,0:T(8,128)(2,1)S(1)} %broadcast_select_fusion.1), channel_id=1, source_target_pairs={{1,0},{2,1},{3,2},{4,3},{5,4},{6,5},{7,6},{8,7},{9,8},{10,9},{11,1... | collective-permute-start | bytes 98312 | tf_op jit(solution)/shard_map/ppermute | solution.py:11
  51.6 5.5 %copy-start.19 = (bf16[512,512]{1,0:T(8,128)(2,1)S(1)}, bf16[512,512]{1,0:T(8,128)(2,1)}, u32[]{:S(2)}) copy-start(bf16[512,512]{1,0:T(8,128)(2,1)} %param.28) | copy-start | bytes 1572868
  55.8 1.3 copy-start.5
  75.1 1.2 copy-start.40
  75.2 1.5 copy-start.22
  76.2 1.0 copy-start.42
  76.2 20.1 %copy-start.30 = (s32[1,1024]{1,0:T(1,128)S(1)}, s32[1,1024]{1,0:T(1,128)}, u32[]{:S(2)}) copy-start(s32[1,1024]{1,0:T(1,128)} %param.25) | copy-start | bytes 12292
  77.2 3.6 copy-start.26
  80.8 30.4 %all-to-all-start = ((bf16[128,8,512]{2,1,0:T(8,128)(2,1)}), bf16[128,8,512]{2,1,0:T(8,128)(2,1)S(1)}, u32[]{:S(2)}, u32[]{:S(2)}) async-start(bf16[128,8,512]{2,1,0:T(8,128)(2,1)} %bitcast.5), calls=%async_computation | async-start | bytes 2097152 | tf_op jit(solution)/shard_map/all_to_all | solution.py:45
  111.2 24.4 %all-to-all-start.2 = ((bf16[128,8,512]{2,1,0:T(8,128)(2,1)}), bf16[128,8,512]{2,1,0:T(8,128)(2,1)}, u32[]{:S(2)}, u32[]{:S(2)}) async-start(bf16[128,8,512]{2,1,0:T(8,128)(2,1)} %bitcast.9), calls=%async_computation.2 | async-start | bytes 2097152 | tf_op jit(solution)/shard_map/all_to_all | solution.py:45
  116.9 18.6 %copy-start.41 = (f32[128]{0:T(128)}, f32[128]{0:T(128)S(1)}, u32[]{:S(2)}) copy-start(f32[128]{0:T(128)S(1)} %broadcast_maximum_fusion) | copy-start | bytes 1540
  117.8 19.2 %copy-start.28 = (bf16[128,512]{1,0:T(8,128)(2,1)}, bf16[128,512]{1,0:T(8,128)(2,1)S(1)}, u32[]{:S(2)}) copy-start(bf16[128,512]{1,0:T(8,128)(2,1)S(1)} %fusion.7) | copy-start | bytes 393220
  137.1 0.7 copy-start.29
  143.1 5.1 %copy-start.37 = (pred[1024]{0:T(1024)(128)(4,1)S(1)}, pred[1024]{0:T(1024)(128)(4,1)}, u32[]{:S(2)}) copy-start(pred[1024]{0:T(1024)(128)(4,1)} %get-tuple-element.31) | copy-start | bytes 3076
  143.1 5.1 %copy-start.38 = (pred[1024]{0:T(1024)(128)(4,1)S(1)}, pred[1024]{0:T(1024)(128)(4,1)}, u32[]{:S(2)}) copy-start(pred[1024]{0:T(1024)(128)(4,1)} %get-tuple-element.32) | copy-start | bytes 3076
  148.2 7.8 %copy-start.34 = (s32[512]{0:T(512)S(1)}, s32[512]{0:T(512)}, u32[]{:S(2)}) copy-start(s32[512]{0:T(512)} %get-tuple-element.18) | copy-start | bytes 6148
  151.1 26.4 %copy-start.35 = (pred[512]{0:T(512)(128)(4,1)S(1)}, pred[512]{0:T(512)(128)(4,1)}, u32[]{:S(2)}) copy-start(pred[512]{0:T(512)(128)(4,1)} %get-tuple-element.17) | copy-start | bytes 1540
  151.1 23.8 %all-to-all-start.3 = ((bf16[128,8,512]{2,1,0:T(8,128)(2,1)}), bf16[128,8,512]{2,1,0:T(8,128)(2,1)S(1)}, u32[]{:S(2)}, u32[]{:S(2)}) async-start(bf16[128,8,512]{2,1,0:T(8,128)(2,1)} %get-tuple-element.33), calls=%async_computation.3 | async-start | bytes 2097152 | tf_op jit(solution)/shard_map/all_to_all | solution.py:45
  155.9 251.3 %all-reduce.3.cloned.1.call-start = ((), (), s32[]{:S(2)}) async-start(), calls=%async_computation.4 | async-start | bytes 14680064 | tf_op jit(solution)/shard_map/psum | solution.py:151
  179.9 0.8 copy-start.24
  180.7 1.3 copy-start.8
  182.1 9.2 %copy-start.31 = (pred[2048]{0:T(1024)(128)(4,1)S(1)}, pred[2048]{0:T(1024)(128)(4,1)}, u32[]{:S(2)}) copy-start(pred[2048]{0:T(1024)(128)(4,1)} %get-tuple-element.47) | copy-start | bytes 6148
  182.1 14.4 %copy-start.20 = (bf16[512,512]{1,0:T(8,128)(2,1)S(1)}, bf16[512,512]{1,0:T(8,128)(2,1)}, u32[]{:S(2)}) copy-start(bf16[512,512]{1,0:T(8,128)(2,1)} %param.28) | copy-start | bytes 1572868
  191.3 5.1 %copy-start.2 = (f32[2048,512]{1,0:T(8,128)S(1)}, f32[2048,512]{1,0:T(8,128)}, u32[]{:S(2)}) copy-start(f32[2048,512]{1,0:T(8,128)} %gather_fusion.1) | copy-start | bytes 12582916
  191.3 6.1 %copy-start.3 = (f32[2048,512]{1,0:T(8,128)S(1)}, f32[2048,512]{1,0:T(8,128)}, u32[]{:S(2)}) copy-start(f32[2048,512]{1,0:T(8,128)} %gather_fusion) | copy-start | bytes 12582916
  191.3 6.1 %copy-start.32 = (pred[2048]{0:T(1024)(128)(4,1)S(1)}, pred[2048]{0:T(1024)(128)(4,1)}, u32[]{:S(2)}) copy-start(pred[2048]{0:T(1024)(128)(4,1)} %get-tuple-element.48) | copy-start | bytes 6148
  195.1 1.3 copy-start.10
  228.9 10.3 %copy-start.6 = (f32[512,512]{1,0:T(8,128)}, f32[512,512]{1,0:T(8,128)S(1)}, u32[]{:S(2)}) copy-start(f32[512,512]{1,0:T(8,128)S(1)} %scatter_custom_fusion.3) | copy-start | bytes 3145732
  228.9 4.9 %copy-start.23 = (bf16[512,512]{1,0:T(8,128)(2,1)S(1)}, bf16[512,512]{1,0:T(8,128)(2,1)}, u32[]{:S(2)}) copy-start(bf16[512,512]{1,0:T(8,128)(2,1)} %copy-done.22) | copy-start | bytes 1572868
  228.9 4.9 %copy-start.25 = (bf16[512,512]{1,0:T(8,128)(2,1)S(1)}, bf16[512,512]{1,0:T(8,128)(2,1)}, u32[]{:S(2)}) copy-start(bf16[512,512]{1,0:T(8,128)(2,1)} %copy-done.24) | copy-start | bytes 1572868
  229.0 7.0 %copy-start.11 = (bf16[512,512]{1,0:T(8,128)(2,1)S(1)}, bf16[512,512]{1,0:T(8,128)(2,1)}, u32[]{:S(2)}) copy-start(bf16[512,512]{1,0:T(8,128)(2,1)} %gather_fusion.10) | copy-start | bytes 1572868
  229.0 7.0 %copy-start.21 = (bf16[512,512]{1,0:T(8,128)(2,1)S(1)}, bf16[512,512]{1,0:T(8,128)(2,1)}, u32[]{:S(2)}) copy-start(bf16[512,512]{1,0:T(8,128)(2,1)} %param.20) | copy-start | bytes 1572868
  229.0 7.0 %copy-start.36 = (pred[512]{0:T(512)(128)(4,1)S(1)}, pred[512]{0:T(512)(128)(4,1)}, u32[]{:S(2)}) copy-start(pred[512]{0:T(512)(128)(4,1)} %get-tuple-element.17) | copy-start | bytes 1540
  229.0 7.0 %copy-start.43 = (f32[512,512]{1,0:T(8,128)S(1)}, f32[512,512]{1,0:T(8,128)}, u32[]{:S(2)}) copy-start(f32[512,512]{1,0:T(8,128)} %copy-done.42) | copy-start | bytes 3145732
  240.7 4.7 %copy-start.33 = (s32[1,4,32]{2,1,0:T(4,128)S(1)}, s32[1,4,32]{2,1,0:T(4,128)}, u32[]{:S(2)}) copy-start(s32[1,4,32]{2,1,0:T(4,128)} %param.23) | copy-start | bytes 1540
  240.7 27.5 %all-to-all-start.1 = ((bf16[128,8,512]{2,1,0:T(8,128)(2,1)}), bf16[128,8,512]{2,1,0:T(8,128)(2,1)S(1)}, u32[]{:S(2)}, u32[]{:S(2)}) async-start(bf16[128,8,512]{2,1,0:T(8,128)(2,1)} %get-tuple-element.34), calls=%async_computation.1 | async-start | bytes 2097152 | tf_op jit(solution)/shard_map/all_to_all | solution.py:45
  268.2 12.5 %copy-start.12 = (bf16[512,512]{1,0:T(8,128)(2,1)S(1)}, bf16[512,512]{1,0:T(8,128)(2,1)}, u32[]{:S(2)}) copy-start(bf16[512,512]{1,0:T(8,128)(2,1)} %gather_fusion.10) | copy-start | bytes 1572868
  270.2 10.6 %copy-start.7 = (f32[512,512]{1,0:T(8,128)S(1)}, f32[512,512]{1,0:T(8,128)}, u32[]{:S(2)}) copy-start(f32[512,512]{1,0:T(8,128)} %copy-done.6) | copy-start | bytes 3145732
  270.2 10.6 %copy-start.9 = (f32[512,1024]{1,0:T(8,128)S(1)}, f32[512,1024]{1,0:T(8,128)}, u32[]{:S(2)}) copy-start(f32[512,1024]{1,0:T(8,128)} %copy-done.8) | copy-start | bytes 6291460
  270.2 10.6 %copy-start.14 = (bf16[512,512]{1,0:T(8,128)(2,1)S(1)}, bf16[512,512]{1,0:T(8,128)(2,1)}, u32[]{:S(2)}) copy-start(bf16[512,512]{1,0:T(8,128)(2,1)} %param.27) | copy-start | bytes 1572868
  270.2 12.2 %copy-start.27 = (bf16[512,512]{1,0:T(8,128)(2,1)S(1)}, bf16[512,512]{1,0:T(8,128)(2,1)}, u32[]{:S(2)}) copy-start(bf16[512,512]{1,0:T(8,128)(2,1)} %copy-done.26) | copy-start | bytes 1572868
  272.0 11.5 %collective-permute-start.7 = (bf16[32,512]{1,0:T(8,128)(2,1)S(1)}, bf16[32,512]{1,0:T(8,128)(2,1)S(1)}, u32[]{:S(2)}, u32[]{:S(2)}) collective-permute-start(bf16[32,512]{1,0:T(8,128)(2,1)S(1)} %get-tuple-element.28), channel_id=1, source_target_pairs={{0,1},{1,2},{2,3},{3,4},{4,5},{5,6},{6,7},{7,8},{8,9},{9,10},{10,1... | collective-permute-start | bytes 98312 | tf_op jit(solution)/shard_map/ppermute | solution.py:11
  274.4 9.1 %collective-permute-start.6 = (bf16[32,512]{1,0:T(8,128)(2,1)S(1)}, bf16[32,512]{1,0:T(8,128)(2,1)S(1)}, u32[]{:S(2)}, u32[]{:S(2)}) collective-permute-start(bf16[32,512]{1,0:T(8,128)(2,1)S(1)} %get-tuple-element.29), channel_id=1, source_target_pairs={{1,0},{2,1},{3,2},{4,3},{5,4},{6,5},{7,6},{8,7},{9,8},{10,9},{11,1... | collective-permute-start | bytes 98312 | tf_op jit(solution)/shard_map/ppermute | solution.py:11
  275.7 7.8 %collective-permute-start.5 = (bf16[32,512]{1,0:T(8,128)(2,1)S(1)}, bf16[32,512]{1,0:T(8,128)(2,1)S(1)}, u32[]{:S(2)}, u32[]{:S(2)}) collective-permute-start(bf16[32,512]{1,0:T(8,128)(2,1)S(1)} %get-tuple-element.30), channel_id=1, source_target_pairs={{0,16},{16,32},{32,48},{48,64},{64,80},{80,96},{96,112},{1,17},{17... | collective-permute-start | bytes 98312 | tf_op jit(solution)/shard_map/ppermute | solution.py:11
  278.8 5.2 %collective-permute-start.4 = (bf16[32,512]{1,0:T(8,128)(2,1)S(1)}, bf16[32,512]{1,0:T(8,128)(2,1)S(1)}, u32[]{:S(2)}, u32[]{:S(2)}) collective-permute-start(bf16[32,512]{1,0:T(8,128)(2,1)S(1)} %get-tuple-element.27), channel_id=1, source_target_pairs={{16,0},{32,16},{48,32},{64,48},{80,64},{96,80},{112,96},{17,1},{33... | collective-permute-start | bytes 98312 | tf_op jit(solution)/shard_map/ppermute | solution.py:11
  285.8 128.8 %copy-start.18 = (f32[512,512]{1,0:T(8,128)}, f32[512,512]{1,0:T(8,128)S(1)}, u32[]{:S(2)}) copy-start(f32[512,512]{1,0:T(8,128)S(1)} %scatter_custom_fusion.5) | copy-start | bytes 3145732
  407.2 4.8 %copy-start.17 = (f32[512,512]{1,0:T(8,128)S(1)}, f32[512,512]{1,0:T(8,128)}, u32[]{:S(2)}) copy-start(f32[512,512]{1,0:T(8,128)} %get-tuple-element.13) | copy-start | bytes 3145732
  407.2 5.9 %copy-start.13 = (f32[1024,512]{1,0:T(8,128)S(1)}, f32[1024,512]{1,0:T(8,128)}, u32[]{:S(2)}) copy-start(f32[1024,512]{1,0:T(8,128)} %get-tuple-element.14) | copy-start | bytes 6291460
  409.6 5.0 %copy-start.16 = (f32[512,512]{1,0:T(8,128)S(1)}, f32[512,512]{1,0:T(8,128)}, u32[]{:S(2)}) copy-start(f32[512,512]{1,0:T(8,128)} %get-tuple-element.15) | copy-start | bytes 3145732
  412.0 3.7 copy-start.15
  413.1 3.7 copy-start.1
Sparse Core Ops, SparseCore 0:
  240.8 166.3 all-reduce.2
where the time goes:
time: 425 us; the launch traced here: 424 us
  waiting for transfers between devices  192 us (45%)
  other arithmetic  69.8 us (16%)
  local copies, waits for them, and re-layouts  62 us (15%)
  starting transfers between devices  46.9 us (11%)
  matrix products  38 us (9%)
  between operations  14.8 us (3%)
    psum x1, waiting for transfers between devices, local(): lax.psum((source_gradient, target_gradient, edge_gradient, inner_gradient...  121 us
    all_to_all x4, waiting for transfers between devices, trade_slots(): lax.all_to_all(buffer, ('row', 'col'), split_axis=0, concat_axis=0, tiled...  70.4 us
    all_to_all x4, starting transfers between devices, trade_slots(): lax.all_to_all(buffer, ('row', 'col'), split_axis=0, concat_axis=0, tiled...  26.8 us
    ppermute x8, starting transfers between devices, passed_along(): lax.ppermute(value, axis, [(source, source + steps) for source in range(i...  20 us
    scatter-add x1, other arithmetic, local(): jax.ops.segment_sum(jax.nn.silu(message_linear), edge_target, count_rows)  14.6 us
    dot_general x6, matrix products, left_product(): lax.dot_general(first, second, (((0,), (0,)), ((), ())), preferred_elemen...  13.9 us
    scatter-add x1, other arithmetic, local(): jax.ops.segment_sum(grad_edges, edge_target, count_rows)  13.7 us
    scatter-add x1, other arithmetic, local(): jax.ops.segment_sum(grad_edges, edge_source, extended.shape[0])  13.6 us
  transfers between devices with their start and end apart: 13, of which 6 were waited for; matrix products, arithmetic and copies ran while one was open for 9% of the time, Pallas kernels for 0%

commit v1 on v0

--- a/solution.py
+++ b/solution.py
@@ -149,15 +149,18 @@
         outer_gradient,
         coarse_gradient,
     ) = lax.psum(
-        (
-            source_gradient,
-            target_gradient,
-            edge_gradient,
-            inner_gradient,
-            outer_gradient,
-            coarse_gradient,
+        lax.psum(
+            (
+                source_gradient,
+                target_gradient,
+                edge_gradient,
+                inner_gradient,
+                outer_gradient,
+                coarse_gradient,
+            ),
+            "col",
         ),
-        ("row", "col"),
+        "row",
     )
     grad_extended = right_product(grad_sources, source_weight)
     back_blocks = grad_extended[count_rows:].astype(jnp.bfloat16).reshape(4, halo_rows, width)

time: 425 us -> 492 us (1.16)
  waiting for transfers between devices: 192 us -> 255 us
    psum x0 -> x1, waiting for transfers between devices: none -> 59.3 us  [local(): lax.psum(lax.psum((source_gradient, target_gradient, edge_gradient, inner...]
    psum x1, waiting for transfers between devices: 121 us -> 128 us  [local(): lax.psum((source_gradient, target_gradient, edge_gradient, inner_gradient...]
  transfers between devices with their start and end apart: 13 -> 14, of which waited for: 6 -> 7; matrix products, arithmetic and copies ran while one was open for 9% -> 7% of each run, Pallas kernels for 0% -> 0%
where the time goes in v1:
time: 492 us; the launch traced here: 491 us
  waiting for transfers between devices  255 us (52%)
  other arithmetic  69.7 us (14%)
  local copies, waits for them, and re-layouts  62 us (13%)
  starting transfers between devices  51.4 us (10%)
  matrix products  37.9 us (8%)
  between operations  14.8 us (3%)
    psum x1, waiting for transfers between devices, local(): lax.psum((source_gradient, target_gradient, edge_gradient, inner_gradient...  128 us
    all_to_all x4, waiting for transfers between devices, trade_slots(): lax.all_to_all(buffer, ('row', 'col'), split_axis=0, concat_axis=0, tiled...  66.4 us
    psum x1, waiting for transfers between devices, local(): lax.psum(lax.psum((source_gradient, target_gradient, edge_gradient, inner...  59.3 us
    all_to_all x4, starting transfers between devices, trade_slots(): lax.all_to_all(buffer, ('row', 'col'), split_axis=0, concat_axis=0, tiled...  30.4 us
    ppermute x8, starting transfers between devices, passed_along(): lax.ppermute(value, axis, [(source, source + steps) for source in range(i...  20.8 us
    scatter-add x1, other arithmetic, local(): jax.ops.segment_sum(jax.nn.silu(message_linear), edge_target, count_rows)  14.6 us
    dot_general x6, matrix products, left_product(): lax.dot_general(first, second, (((0,), (0,)), ((), ())), preferred_elemen...  13.9 us
    scatter-add x1, other arithmetic, local(): jax.ops.segment_sum(grad_edges, edge_target, count_rows)  13.7 us
  transfers between devices with their start and end apart: 14, of which 7 were waited for; matrix products, arithmetic and copies ran while one was open for 7% of the time, Pallas kernels for 0%

profile of v1, /device:TPU:1, one launch (start us, length us, event | category | flops | bytes accessed | tf_op | source)
XLA Modules:
  0.0 490.6 jit_solution(6487926562509666258)
XLA Ops:
  8.1 1.7 gather_fusion.3
  9.9 4.9 %collective-permute-start = (bf16[32,512]{1,0:T(8,128)(2,1)S(1)}, bf16[32,512]{1,0:T(8,128)(2,1)S(1)}, u32[]{:S(2)}, u32[]{:S(2)}) collective-permute-start(bf16[32,512]{1,0:T(8,128)(2,1)S(1)} %broadcast_select_fusion.4), channel_id=1, source_target_pairs={{0,16},{16,32},{32,48},{48,64},{64,80},{80,96},{96,112},{1,17},{17... | collective-permute-start | bytes 98312 | tf_op jit(solution)/shard_map/ppermute | solution.py:11
  14.8 1.7 gather_fusion.4
  16.7 1.9 collective-permute-start.1
  18.6 1.7 gather_fusion.5
  20.4 3.2 collective-permute-start.2
  23.6 1.7 gather_fusion.6
  25.5 1.3 collective-permute-start.3
  27.5 1.3 compare_and_fusion
  28.8 1.6 fusion.57
  32.1 8.9 %gather_fusion.1 = f32[2048,512]{1,0:T(8,128)} fusion(f32[512,512]{1,0:T(8,128)S(1)} %fusion.57, s32[2048]{0:T(1024)S(1)} %get-tuple-element.52), kind=kCustom, calls=%fused_computation.9 | custom fusion | bytes 8396800 | tf_op jit(solution)/shard_map/jit(_take)/gather | solution.py:90
  41.1 1.5 fusion.56
  42.6 9.0 %gather_fusion = f32[2048,512]{1,0:T(8,128)} fusion(f32[640,512]{1,0:T(8,128)S(1)} %fusion.56, s32[2048]{0:T(1024)S(1)} %get-tuple-element.51), kind=kCustom, calls=%fused_computation.8 | custom fusion | bytes 8396800 | tf_op jit(solution)/shard_map/jit(_take)/gather | solution.py:90
  51.6 4.2 multiply_convert_fusion.1
  55.9 1.3 copy-done.5
  57.1 3.3 fusion.58
  60.5 14.6 %scatter_custom_fusion = f32[512,512]{1,0:T(8,128)S(1)} fusion(s32[2048]{0:T(1024)} %param.22, f32[2048,512]{1,0:T(8,128)} %fusion.58, f32[]{:T(128)} %constant.62.clone.1, f32[]{:T(128)} %constant.52.clone.1), kind=kCustom, calls=%fused_computation.19 | custom fusion | flops 5242880 | bytes 5243904 | tf_op jit(solution)/shard_map/scatter-add | solution.py:95
  77.2 3.6 scatter_custom_fusion.1
  80.8 11.6 %all-to-all-start = ((bf16[128,8,512]{2,1,0:T(8,128)(2,1)}), bf16[128,8,512]{2,1,0:T(8,128)(2,1)S(1)}, u32[]{:S(2)}, u32[]{:S(2)}) async-start(bf16[128,8,512]{2,1,0:T(8,128)(2,1)} %bitcast.5), calls=%async_computation | async-start | bytes 2097152 | tf_op jit(solution)/shard_map/all_to_all | solution.py:45
  92.4 4.0 scatter_custom_fusion.2
  96.5 14.7 %all-to-all-done = bf16[128,8,512]{2,1,0:T(8,128)(2,1)S(1)} async-done(((bf16[128,8,512]{2,1,0:T(8,128)(2,1)}), bf16[128,8,512]{2,1,0:T(8,128)(2,1)S(1)}, u32[]{:S(2)}, u32[]{:S(2)}) %all-to-all-start) | async-done | bytes 1048608 | tf_op jit(solution)/shard_map/all_to_all | solution.py:45
  111.2 5.7 %all-to-all-start.2 = ((bf16[128,8,512]{2,1,0:T(8,128)(2,1)}), bf16[128,8,512]{2,1,0:T(8,128)(2,1)}, u32[]{:S(2)}, u32[]{:S(2)}) async-start(bf16[128,8,512]{2,1,0:T(8,128)(2,1)} %bitcast.9), calls=%async_computation.2 | async-start | bytes 2097152 | tf_op jit(solution)/shard_map/all_to_all | solution.py:45
  117.9 1.4 multiply_convert_fusion.3
  119.2 16.3 %all-to-all-done.2 = bf16[128,8,512]{2,1,0:T(8,128)(2,1)} async-done(((bf16[128,8,512]{2,1,0:T(8,128)(2,1)}), bf16[128,8,512]{2,1,0:T(8,128)(2,1)}, u32[]{:S(2)}, u32[]{:S(2)}) %all-to-all-start.2) | async-done | bytes 1048608 | tf_op jit(solution)/shard_map/all_to_all | solution.py:45
  135.6 1.5 fusion.8
  137.8 1.4 fusion.6
  139.1 4.0 gather_fusion.9
  143.1 5.1 %gather_fusion.7 = bf16[1024,512]{1,0:T(8,128)(2,1)} fusion(bf16[128,512]{1,0:T(8,128)(2,1)S(1)} %get-tuple-element.47, s32[1024]{0:T(1024)S(1)} %maximum_clamp_fusion), kind=kCustom, calls=%fused_computation.1.clone | custom fusion | bytes 2101248 | tf_op jit(solution)/shard_map/jit(_take)/gather | solution.py:57
  148.2 2.9 fusion.12
  151.1 4.8 all-to-all-start.3
  156.0 2.3 fusion.61
  158.3 16.6 %all-to-all-done.3 = bf16[128,8,512]{2,1,0:T(8,128)(2,1)S(1)} async-done(((bf16[128,8,512]{2,1,0:T(8,128)(2,1)}), bf16[128,8,512]{2,1,0:T(8,128)(2,1)S(1)}, u32[]{:S(2)}, u32[]{:S(2)}) %all-to-all-start.3) | async-done | bytes 1048608 | tf_op jit(solution)/shard_map/all_to_all | solution.py:45
  174.9 2.6 gather_fusion.10
  177.5 2.4 fusion.5
  180.7 1.3 copy-done.8
  182.1 9.2 %gather_fusion.2 = bf16[2048,512]{1,0:T(8,128)(2,1)} fusion(bf16[512,512]{1,0:T(8,128)(2,1)S(1)} %slice.97, s32[2048]{0:T(1024)S(1)} %get-tuple-element.52), kind=kCustom, calls=%fused_computation.10 | custom fusion | bytes 4202496 | tf_op jit(solution)/shard_map/jit(_take)/gather | solution.py:134
  191.3 3.8 multiply_convert_fusion
  195.2 1.3 copy-done.10
  197.4 4.3 multiply_multiply_fusion
  201.7 13.6 %scatter_custom_fusion.4 = f32[640,512]{1,0:T(8,128)S(1)} fusion(s32[2048]{0:T(1024)} %param.21, f32[2048,512]{1,0:T(8,128)} %multiply_multiply_fusion, f32[]{:T(128)} %constant.52.clone.1), kind=kCustom, calls=%fused_computation.59 | custom fusion | flops 1048576 | bytes 1311232 | tf_op jit(solution)/shard_map/scatter-add | solution.py:138
  215.2 13.7 %scatter_custom_fusion.3 = f32[512,512]{1,0:T(8,128)S(1)} fusion(s32[2048]{0:T(1024)} %param.22, f32[2048,512]{1,0:T(8,128)} %multiply_multiply_fusion, f32[]{:T(128)} %constant.52.clone.1), kind=kCustom, calls=%fused_computation.73 | custom fusion | flops 1048576 | bytes 1049088 | tf_op jit(solution)/shard_map/scatter-add | solution.py:141
  229.0 4.9 fusion.60
  233.9 2.1 fusion.15
  236.0 1.7 fusion.51
  237.7 1.6 fusion.27
  239.2 1.5 convolution_bitcast_fusion
  240.8 127.6 %all-reduce.5.cloned.1.call-done = (f32[512,512]{1,0:T(8,128)}, f32[512,512]{1,0:T(8,128)}, f32[512,512]{1,0:T(8,128)}, f32[1024,512]{1,0:T(8,128)}, f32[512,512]{1,0:T(8,128)}, /*index=5*/f32[512,512]{1,0:T(8,128)}) async-done(((f32[512,512]{1,0:T(8,128)}, f32[512,512]{1,0:T(8,128)}, f32[512,512]{1,0:T(8,128)}, f32[1024,512]{1,0:T(8,128)}, f32[512,512]{1,0:T(8,128)}, /*index=5*/f32[512,512]{1,0:T(8,128)}), ...) | async-done | bytes 7340048 | tf_op jit(solution)/shard_map/psum | solution.py:152
  368.4 8.3 %all-to-all-start.1 = ((bf16[128,8,512]{2,1,0:T(8,128)(2,1)}), bf16[128,8,512]{2,1,0:T(8,128)(2,1)S(1)}, u32[]{:S(2)}, u32[]{:S(2)}) async-start(bf16[128,8,512]{2,1,0:T(8,128)(2,1)} %get-tuple-element.40), calls=%async_computation.1 | async-start | bytes 2097152 | tf_op jit(solution)/shard_map/all_to_all | solution.py:45
  376.8 18.7 %all-to-all-done.1 = bf16[128,8,512]{2,1,0:T(8,128)(2,1)S(1)} async-done(((bf16[128,8,512]{2,1,0:T(8,128)(2,1)}), bf16[128,8,512]{2,1,0:T(8,128)(2,1)S(1)}, u32[]{:S(2)}, u32[]{:S(2)}) %all-to-all-start.1) | async-done | bytes 1048608 | tf_op jit(solution)/shard_map/all_to_all | solution.py:45
  395.6 2.0 gather_fusion.8
  397.6 1.7 fusion.55
  399.4 2.1 collective-permute-start.7
  401.5 1.3 collective-permute-start.6
  402.8 4.2 collective-permute-start.5
  407.0 1.9 collective-permute-start.4
  409.0 1.6 fusion.3
  411.7 1.4 collective-permute-done.4
  413.1 1.8 scatter_custom_fusion.5
  414.8 59.3 %all-reduce.7.cloned.1.call-done = (f32[512,512]{1,0:T(8,128)}, f32[512,512]{1,0:T(8,128)}, f32[512,512]{1,0:T(8,128)}, f32[1024,512]{1,0:T(8,128)}, f32[512,512]{1,0:T(8,128)}, /*index=5*/f32[512,512]{1,0:T(8,128)}) async-done(((f32[512,512]{1,0:T(8,128)}, f32[512,512]{1,0:T(8,128)}, f32[512,512]{1,0:T(8,128)}, f32[1024,512]{1,0:T(8,128)}, f32[512,512]{1,0:T(8,128)}, /*index=5*/f32[512,512]{1,0:T(8,128)}), ...) | async-done | bytes 7340048 | tf_op jit(solution)/shard_map/psum | solution.py:151
  474.2 2.4 broadcast_multiply_fusion.5
  476.6 2.4 broadcast_multiply_fusion.4
  480.1 1.5 broadcast_multiply_fusion
  481.6 1.1 broadcast_multiply_fusion.2
  482.7 1.1 broadcast_multiply_fusion.1
  (129 shorter events, 11.7 us)
Async XLA Ops:
  7.2 68.0 %copy-start = (bf16[1024,512]{1,0:T(8,128)(2,1)S(1)}, bf16[1024,512]{1,0:T(8,128)(2,1)}, u32[]{:S(2)}) copy-start(bf16[1024,512]{1,0:T(8,128)(2,1)} %param.29) | copy-start | bytes 3145732
  7.2 24.9 %copy-start.4 = (bf16[512,512]{1,0:T(8,128)(2,1)S(1)}, bf16[512,512]{1,0:T(8,128)(2,1)}, u32[]{:S(2)}) copy-start(bf16[512,512]{1,0:T(8,128)(2,1)} %param.19) | copy-start | bytes 1572868
  7.2 24.3 %copy-start.39 = (s32[512]{0:T(512)S(1)}, s32[512]{0:T(512)}, u32[]{:S(2)}) copy-start(s32[512]{0:T(512)} %param.24) | copy-start | bytes 6148
  9.9 31.1 %collective-permute-start = (bf16[32,512]{1,0:T(8,128)(2,1)S(1)}, bf16[32,512]{1,0:T(8,128)(2,1)S(1)}, u32[]{:S(2)}, u32[]{:S(2)}) collective-permute-start(bf16[32,512]{1,0:T(8,128)(2,1)S(1)} %broadcast_select_fusion.4), channel_id=1, source_target_pairs={{0,16},{16,32},{32,48},{48,64},{64,80},{80,96},{96,112},{1,17},{17... | collective-permute-start | bytes 98312 | tf_op jit(solution)/shard_map/ppermute | solution.py:11
  16.7 24.4 %collective-permute-start.1 = (bf16[32,512]{1,0:T(8,128)(2,1)S(1)}, bf16[32,512]{1,0:T(8,128)(2,1)S(1)}, u32[]{:S(2)}, u32[]{:S(2)}) collective-permute-start(bf16[32,512]{1,0:T(8,128)(2,1)S(1)} %broadcast_select_fusion.3), channel_id=1, source_target_pairs={{16,0},{32,16},{48,32},{64,48},{80,64},{96,80},{112,96},{17,1},{33... | collective-permute-start | bytes 98312 | tf_op jit(solution)/shard_map/ppermute | solution.py:11
  20.4 20.6 %collective-permute-start.2 = (bf16[32,512]{1,0:T(8,128)(2,1)S(1)}, bf16[32,512]{1,0:T(8,128)(2,1)S(1)}, u32[]{:S(2)}, u32[]{:S(2)}) collective-permute-start(bf16[32,512]{1,0:T(8,128)(2,1)S(1)} %broadcast_select_fusion.2), channel_id=1, source_target_pairs={{0,1},{1,2},{2,3},{3,4},{4,5},{5,6},{6,7},{7,8},{8,9},{9,10},{10,1... | collective-permute-start | bytes 98312 | tf_op jit(solution)/shard_map/ppermute | solution.py:11
  25.5 15.6 %collective-permute-start.3 = (bf16[32,512]{1,0:T(8,128)(2,1)S(1)}, bf16[32,512]{1,0:T(8,128)(2,1)S(1)}, u32[]{:S(2)}, u32[]{:S(2)}) collective-permute-start(bf16[32,512]{1,0:T(8,128)(2,1)S(1)} %broadcast_select_fusion.1), channel_id=1, source_target_pairs={{1,0},{2,1},{3,2},{4,3},{5,4},{6,5},{7,6},{8,7},{9,8},{10,9},{11,1... | collective-permute-start | bytes 98312 | tf_op jit(solution)/shard_map/ppermute | solution.py:11
  51.6 5.6 %copy-start.19 = (bf16[512,512]{1,0:T(8,128)(2,1)S(1)}, bf16[512,512]{1,0:T(8,128)(2,1)}, u32[]{:S(2)}) copy-start(bf16[512,512]{1,0:T(8,128)(2,1)} %param.28) | copy-start | bytes 1572868
  55.8 1.3 copy-start.5
  75.1 1.2 copy-start.40
  75.2 1.5 copy-start.22
  76.2 1.0 copy-start.42
  76.2 20.1 %copy-start.30 = (s32[1,1024]{1,0:T(1,128)S(1)}, s32[1,1024]{1,0:T(1,128)}, u32[]{:S(2)}) copy-start(s32[1,1024]{1,0:T(1,128)} %param.25) | copy-start | bytes 12292
  77.2 3.6 copy-start.26
  80.8 30.4 %all-to-all-start = ((bf16[128,8,512]{2,1,0:T(8,128)(2,1)}), bf16[128,8,512]{2,1,0:T(8,128)(2,1)S(1)}, u32[]{:S(2)}, u32[]{:S(2)}) async-start(bf16[128,8,512]{2,1,0:T(8,128)(2,1)} %bitcast.5), calls=%async_computation | async-start | bytes 2097152 | tf_op jit(solution)/shard_map/all_to_all | solution.py:45
  111.2 24.4 %all-to-all-start.2 = ((bf16[128,8,512]{2,1,0:T(8,128)(2,1)}), bf16[128,8,512]{2,1,0:T(8,128)(2,1)}, u32[]{:S(2)}, u32[]{:S(2)}) async-start(bf16[128,8,512]{2,1,0:T(8,128)(2,1)} %bitcast.9), calls=%async_computation.2 | async-start | bytes 2097152 | tf_op jit(solution)/shard_map/all_to_all | solution.py:45
  117.0 18.6 %copy-start.41 = (f32[128]{0:T(128)}, f32[128]{0:T(128)S(1)}, u32[]{:S(2)}) copy-start(f32[128]{0:T(128)S(1)} %broadcast_maximum_fusion) | copy-start | bytes 1540
  117.9 19.2 %copy-start.28 = (bf16[128,512]{1,0:T(8,128)(2,1)}, bf16[128,512]{1,0:T(8,128)(2,1)S(1)}, u32[]{:S(2)}) copy-start(bf16[128,512]{1,0:T(8,128)(2,1)S(1)} %fusion.7) | copy-start | bytes 393220
  137.1 0.7 copy-start.29
  143.1 5.1 %copy-start.37 = (pred[1024]{0:T(1024)(128)(4,1)S(1)}, pred[1024]{0:T(1024)(128)(4,1)}, u32[]{:S(2)}) copy-start(pred[1024]{0:T(1024)(128)(4,1)} %get-tuple-element.37) | copy-start | bytes 3076
  143.1 5.1 %copy-start.38 = (pred[1024]{0:T(1024)(128)(4,1)S(1)}, pred[1024]{0:T(1024)(128)(4,1)}, u32[]{:S(2)}) copy-start(pred[1024]{0:T(1024)(128)(4,1)} %get-tuple-element.38) | copy-start | bytes 3076
  148.2 7.8 %copy-start.34 = (s32[512]{0:T(512)S(1)}, s32[512]{0:T(512)}, u32[]{:S(2)}) copy-start(s32[512]{0:T(512)} %get-tuple-element.24) | copy-start | bytes 6148
  151.1 26.4 %copy-start.35 = (pred[512]{0:T(512)(128)(4,1)S(1)}, pred[512]{0:T(512)(128)(4,1)}, u32[]{:S(2)}) copy-start(pred[512]{0:T(512)(128)(4,1)} %get-tuple-element.23) | copy-start | bytes 1540
  151.1 23.8 %all-to-all-start.3 = ((bf16[128,8,512]{2,1,0:T(8,128)(2,1)}), bf16[128,8,512]{2,1,0:T(8,128)(2,1)S(1)}, u32[]{:S(2)}, u32[]{:S(2)}) async-start(bf16[128,8,512]{2,1,0:T(8,128)(2,1)} %get-tuple-element.39), calls=%async_computation.3 | async-start | bytes 2097152 | tf_op jit(solution)/shard_map/all_to_all | solution.py:45
  155.9 212.5 %all-reduce.5.cloned.1.call-start = ((), (), s32[]{:S(2)}) async-start(), calls=%async_computation.4 | async-start | bytes 14680064 | tf_op jit(solution)/shard_map/psum | solution.py:152
  179.9 0.8 copy-start.24
  180.7 1.3 copy-start.8
  182.1 9.2 %copy-start.31 = (pred[2048]{0:T(1024)(128)(4,1)S(1)}, pred[2048]{0:T(1024)(128)(4,1)}, u32[]{:S(2)}) copy-start(pred[2048]{0:T(1024)(128)(4,1)} %get-tuple-element.53) | copy-start | bytes 6148
  182.1 14.4 %copy-start.20 = (bf16[512,512]{1,0:T(8,128)(2,1)S(1)}, bf16[512,512]{1,0:T(8,128)(2,1)}, u32[]{:S(2)}) copy-start(bf16[512,512]{1,0:T(8,128)(2,1)} %param.28) | copy-start | bytes 1572868
  191.3 5.1 %copy-start.2 = (f32[2048,512]{1,0:T(8,128)S(1)}, f32[2048,512]{1,0:T(8,128)}, u32[]{:S(2)}) copy-start(f32[2048,512]{1,0:T(8,128)} %gather_fusion.1) | copy-start | bytes 12582916
  191.3 6.1 %copy-start.3 = (f32[2048,512]{1,0:T(8,128)S(1)}, f32[2048,512]{1,0:T(8,128)}, u32[]{:S(2)}) copy-start(f32[2048,512]{1,0:T(8,128)} %gather_fusion) | copy-start | bytes 12582916
  191.3 6.1 %copy-start.32 = (pred[2048]{0:T(1024)(128)(4,1)S(1)}, pred[2048]{0:T(1024)(128)(4,1)}, u32[]{:S(2)}) copy-start(pred[2048]{0:T(1024)(128)(4,1)} %get-tuple-element.54) | copy-start | bytes 6148
  195.1 1.3 copy-start.10
  229.0 10.3 %copy-start.6 = (f32[512,512]{1,0:T(8,128)}, f32[512,512]{1,0:T(8,128)S(1)}, u32[]{:S(2)}) copy-start(f32[512,512]{1,0:T(8,128)S(1)} %scatter_custom_fusion.3) | copy-start | bytes 3145732
  229.0 4.9 %copy-start.23 = (bf16[512,512]{1,0:T(8,128)(2,1)S(1)}, bf16[512,512]{1,0:T(8,128)(2,1)}, u32[]{:S(2)}) copy-start(bf16[512,512]{1,0:T(8,128)(2,1)} %copy-done.22) | copy-start | bytes 1572868
  229.0 4.9 %copy-start.25 = (bf16[512,512]{1,0:T(8,128)(2,1)S(1)}, bf16[512,512]{1,0:T(8,128)(2,1)}, u32[]{:S(2)}) copy-start(bf16[512,512]{1,0:T(8,128)(2,1)} %copy-done.24) | copy-start | bytes 1572868
  229.0 7.0 %copy-start.11 = (bf16[512,512]{1,0:T(8,128)(2,1)S(1)}, bf16[512,512]{1,0:T(8,128)(2,1)}, u32[]{:S(2)}) copy-start(bf16[512,512]{1,0:T(8,128)(2,1)} %gather_fusion.10) | copy-start | bytes 1572868
  229.0 7.0 %copy-start.21 = (bf16[512,512]{1,0:T(8,128)(2,1)S(1)}, bf16[512,512]{1,0:T(8,128)(2,1)}, u32[]{:S(2)}) copy-start(bf16[512,512]{1,0:T(8,128)(2,1)} %param.20) | copy-start | bytes 1572868
  229.0 7.0 %copy-start.36 = (pred[512]{0:T(512)(128)(4,1)S(1)}, pred[512]{0:T(512)(128)(4,1)}, u32[]{:S(2)}) copy-start(pred[512]{0:T(512)(128)(4,1)} %get-tuple-element.23) | copy-start | bytes 1540
  229.0 7.0 %copy-start.43 = (f32[512,512]{1,0:T(8,128)S(1)}, f32[512,512]{1,0:T(8,128)}, u32[]{:S(2)}) copy-start(f32[512,512]{1,0:T(8,128)} %copy-done.42) | copy-start | bytes 3145732
  240.7 233.4 %all-reduce.7.cloned.1.call-start = ((), (), s32[]{:S(2)}) async-start(), calls=%async_computation.5 | async-start | bytes 14680064 | tf_op jit(solution)/shard_map/psum | solution.py:151
  368.4 8.4 %copy-start.33 = (s32[1,4,32]{2,1,0:T(4,128)S(1)}, s32[1,4,32]{2,1,0:T(4,128)}, u32[]{:S(2)}) copy-start(s32[1,4,32]{2,1,0:T(4,128)} %param.23) | copy-start | bytes 1540
  368.4 27.2 %all-to-all-start.1 = ((bf16[128,8,512]{2,1,0:T(8,128)(2,1)}), bf16[128,8,512]{2,1,0:T(8,128)(2,1)S(1)}, u32[]{:S(2)}, u32[]{:S(2)}) async-start(bf16[128,8,512]{2,1,0:T(8,128)(2,1)} %get-tuple-element.40), calls=%async_computation.1 | async-start | bytes 2097152 | tf_op jit(solution)/shard_map/all_to_all | solution.py:45
  395.6 13.4 %copy-start.12 = (bf16[512,512]{1,0:T(8,128)(2,1)S(1)}, bf16[512,512]{1,0:T(8,128)(2,1)}, u32[]{:S(2)}) copy-start(bf16[512,512]{1,0:T(8,128)(2,1)} %gather_fusion.10) | copy-start | bytes 1572868
  397.5 11.4 %copy-start.7 = (f32[512,512]{1,0:T(8,128)S(1)}, f32[512,512]{1,0:T(8,128)}, u32[]{:S(2)}) copy-start(f32[512,512]{1,0:T(8,128)} %copy-done.6) | copy-start | bytes 3145732
  397.6 11.4 %copy-start.9 = (f32[512,1024]{1,0:T(8,128)S(1)}, f32[512,1024]{1,0:T(8,128)}, u32[]{:S(2)}) copy-start(f32[512,1024]{1,0:T(8,128)} %copy-done.8) | copy-start | bytes 6291460
  397.6 11.4 %copy-start.14 = (bf16[512,512]{1,0:T(8,128)(2,1)S(1)}, bf16[512,512]{1,0:T(8,128)(2,1)}, u32[]{:S(2)}) copy-start(bf16[512,512]{1,0:T(8,128)(2,1)} %param.27) | copy-start | bytes 1572868
  397.6 13.0 %copy-start.27 = (bf16[512,512]{1,0:T(8,128)(2,1)S(1)}, bf16[512,512]{1,0:T(8,128)(2,1)}, u32[]{:S(2)}) copy-start(bf16[512,512]{1,0:T(8,128)(2,1)} %copy-done.26) | copy-start | bytes 1572868
  399.4 12.3 %collective-permute-start.7 = (bf16[32,512]{1,0:T(8,128)(2,1)S(1)}, bf16[32,512]{1,0:T(8,128)(2,1)S(1)}, u32[]{:S(2)}, u32[]{:S(2)}) collective-permute-start(bf16[32,512]{1,0:T(8,128)(2,1)S(1)} %get-tuple-element.34), channel_id=1, source_target_pairs={{0,1},{1,2},{2,3},{3,4},{4,5},{5,6},{6,7},{7,8},{8,9},{9,10},{10,1... | collective-permute-start | bytes 98312 | tf_op jit(solution)/shard_map/ppermute | solution.py:11
  401.5 10.1 %collective-permute-start.6 = (bf16[32,512]{1,0:T(8,128)(2,1)S(1)}, bf16[32,512]{1,0:T(8,128)(2,1)S(1)}, u32[]{:S(2)}, u32[]{:S(2)}) collective-permute-start(bf16[32,512]{1,0:T(8,128)(2,1)S(1)} %get-tuple-element.35), channel_id=1, source_target_pairs={{1,0},{2,1},{3,2},{4,3},{5,4},{6,5},{7,6},{8,7},{9,8},{10,9},{11,1... | collective-permute-start | bytes 98312 | tf_op jit(solution)/shard_map/ppermute | solution.py:11
  402.8 8.9 %collective-permute-start.5 = (bf16[32,512]{1,0:T(8,128)(2,1)S(1)}, bf16[32,512]{1,0:T(8,128)(2,1)S(1)}, u32[]{:S(2)}, u32[]{:S(2)}) collective-permute-start(bf16[32,512]{1,0:T(8,128)(2,1)S(1)} %get-tuple-element.36), channel_id=1, source_target_pairs={{0,16},{16,32},{32,48},{48,64},{64,80},{80,96},{96,112},{1,17},{17... | collective-permute-start | bytes 98312 | tf_op jit(solution)/shard_map/ppermute | solution.py:11
  407.0 6.0 %collective-permute-start.4 = (bf16[32,512]{1,0:T(8,128)(2,1)S(1)}, bf16[32,512]{1,0:T(8,128)(2,1)S(1)}, u32[]{:S(2)}, u32[]{:S(2)}) collective-permute-start(bf16[32,512]{1,0:T(8,128)(2,1)S(1)} %get-tuple-element.33), channel_id=1, source_target_pairs={{16,0},{32,16},{48,32},{64,48},{80,64},{96,80},{112,96},{17,1},{33... | collective-permute-start | bytes 98312 | tf_op jit(solution)/shard_map/ppermute | solution.py:11
  414.8 66.8 %copy-start.18 = (f32[512,512]{1,0:T(8,128)}, f32[512,512]{1,0:T(8,128)S(1)}, u32[]{:S(2)}) copy-start(f32[512,512]{1,0:T(8,128)S(1)} %scatter_custom_fusion.5) | copy-start | bytes 3145732
  474.2 4.8 copy-start.17
  474.2 5.9 %copy-start.13 = (f32[1024,512]{1,0:T(8,128)S(1)}, f32[1024,512]{1,0:T(8,128)}, u32[]{:S(2)}) copy-start(f32[1024,512]{1,0:T(8,128)} %get-tuple-element.20) | copy-start | bytes 6291460
  476.6 5.0 %copy-start.16 = (f32[512,512]{1,0:T(8,128)S(1)}, f32[512,512]{1,0:T(8,128)}, u32[]{:S(2)}) copy-start(f32[512,512]{1,0:T(8,128)} %get-tuple-element.21) | copy-start | bytes 3145732
  479.0 3.7 copy-start.15
  480.1 3.7 copy-start.1
Sparse Core Ops, SparseCore 0:
  240.8 127.4 all-reduce.4
  371.2 102.9 all-reduce.6
